TPU v7x, 32 devices: a whole 2x2x4 slice. The times are simulated.
32 devices in a mesh: chan: 8 (over z, y), off: 4 (over x, core).
Axes of the slice: x: 2, y: 2, z: 4, core: 2. Of those that a mesh axis runs over, the one named last changes fastest.
Arguments:
- traces: bfloat16 [512, 4096], P('chan'), may hold values from -6 to 6
- band_gain: float32 [2048], P('off'), may hold values from 0.5 to 2
- pair_list: int32 [2048, 2], P('chan'), may hold values from 0 to 511, as said below
- pair_count: int32 [32], P(('chan', 'off')), may hold values from 16 to 64, as said below
Outputs:
- gathers: float32 [2048, 1024], P(('chan', 'off'))
Inputs may be any that keep to these rules, and one draw needn't show every extreme that they name: `pair_list`: row r names first a channel of block r // 256 (channels c * 64 to c * 64 + 63 form block c), then a channel whose block lies at most 2 blocks away from it around the loop of blocks, either way. Slots that are not live hold pairs of the same kind. `pair_count`: in every channel block one owner has all 64 slots live.
All inputs are finite; a program needn't handle non-finite values.
Results may differ from a plain program's by a relative error of at most 0.0064.
Values may be sent and summed in bfloat16 or wider, within the bound.
A program may use at most 64 MiB of HBM per device.

v0:
```python
import math

import jax
import jax.numpy as jnp
from jax import lax
from jax.sharding import PartitionSpec as P

NLAG = 1024
BAND = 64


def shifted(value, axis, steps):
    count = lax.axis_size(axis)
    pairs = [(source, (source + steps) % count) for source in range(count)]
    return lax.ppermute(value, axis, pairs)


def forward_basis(time_count, bin_lo, bin_count, sample_count):
    sample_ids = jnp.arange(time_count, dtype=jnp.int32)[:, None]
    bin_ids = (bin_lo + jnp.arange(bin_count, dtype=jnp.int32))[None, :]
    angles = jnp.mod(sample_ids * bin_ids, sample_count).astype(jnp.float32) * (
        2.0 * math.pi / sample_count
    )
    return jnp.concatenate([jnp.cos(angles), -jnp.sin(angles)], axis=1).astype(jnp.bfloat16)


def inverse_basis(bin_lo, bin_count, sample_count, lag_count):
    bin_ids = (bin_lo + jnp.arange(bin_count, dtype=jnp.int32))[:, None]
    lag_ids = jnp.arange(lag_count, dtype=jnp.int32)[None, :] - lag_count // 2
    angles = jnp.mod(bin_ids * lag_ids, sample_count).astype(jnp.float32) * (
        2.0 * math.pi / sample_count
    )
    return jnp.concatenate([jnp.cos(angles), -jnp.sin(angles)], axis=0).astype(jnp.bfloat16)


def whiten(raw_spectra, gain):
    bin_count = gain.shape[0]
    row_count = raw_spectra.shape[0]
    real_part = raw_spectra[:, :bin_count]
    imag_part = raw_spectra[:, bin_count:]
    band_power = (real_part * real_part + imag_part * imag_part).reshape(
        row_count, bin_count // BAND, BAND
    )
    band_scale = lax.rsqrt(jnp.mean(band_power, axis=2) + 1e-06)
    band_scale = jnp.repeat(band_scale, BAND, axis=1) * gain[None, :]
    return jnp.concatenate([real_part * band_scale, imag_part * band_scale], axis=1).astype(
        jnp.bfloat16
    )


def cross_spectra(left_rows, right_rows):
    half = left_rows.shape[1] // 2
    left_rows = left_rows.astype(jnp.float32)
    right_rows = right_rows.astype(jnp.float32)
    left_real, left_imag = (left_rows[:, :half], left_rows[:, half:])
    right_real, right_imag = (right_rows[:, :half], right_rows[:, half:])
    real_part = left_real * right_real + left_imag * right_imag
    imag_part = left_real * right_imag - left_imag * right_real
    return jnp.concatenate([real_part, imag_part], axis=1).astype(jnp.bfloat16)


def shards(traces, band_gain, pair_list, pair_count):
    chan_total = lax.axis_size("chan")
    owners = lax.axis_size("off")
    reach_blocks = chan_total // 4
    rows_dev = traces.shape[0]
    sample_count = traces.shape[1]
    bin_count = band_gain.shape[0]
    bin_lo = lax.axis_index("off") * bin_count
    block_index = lax.axis_index("chan")
    dft_basis = forward_basis(sample_count, bin_lo, bin_count, sample_count)
    raw_spectra = jnp.dot(traces, dft_basis, preferred_element_type=jnp.float32)
    own_spectra = whiten(raw_spectra, band_gain)
    lower_side = []
    upper_side = []
    moving = own_spectra
    for hop_index in range(reach_blocks):
        moving = shifted(moving, "chan", 1)
        lower_side.append(moving)
    moving = own_spectra
    for hop_index in range(reach_blocks):
        moving = shifted(moving, "chan", -1)
        upper_side.append(moving)
    local_table = jnp.concatenate(lower_side[::-1] + [own_spectra] + upper_side, axis=0)
    first_row = pair_list[:, 0] % rows_dev + reach_blocks * rows_dev
    partner = pair_list[:, 1]
    position = jnp.mod(partner // rows_dev - block_index + reach_blocks, chan_total)
    second_row = position * rows_dev + partner % rows_dev
    cross = cross_spectra(local_table[first_row], local_table[second_row])
    slot_cap = pair_list.shape[0] // owners
    inverse = inverse_basis(bin_lo, bin_count, sample_count, NLAG)
    lagsum = lax.psum_scatter(
        jnp.dot(cross, inverse, preferred_element_type=jnp.float32),
        "off",
        scatter_dimension=0,
        tiled=True,
    )
    group_count = pair_count.shape[0]
    group_size = slot_cap // group_count
    slot_ids = jnp.arange(slot_cap, dtype=jnp.int32)
    limits = jnp.repeat(pair_count, group_size)
    live_slots = slot_ids % group_size < limits
    return jnp.where(live_slots[:, None], lagsum * (1.0 / math.sqrt(sample_count // 2)), 0.0)


def solution(mesh):
    placed = (P("chan", None), P("off"), P("chan", None), P(("chan", "off")))
    return jax.shard_map(
        shards, mesh=mesh, in_specs=placed, out_specs=P(("chan", "off"), None), check_vma=False
    )
```

profile of v0, /device:TPU:0, one launch (start us, length us, event | category | flops | bytes accessed | tf_op | source)
XLA Modules:
  0.0 107.3 jit_solution(2441479593541748970)
XLA Ops:
  6.5 0.0 copy-start
  6.5 0.0 reduce-scatter.2.cloned.1.call-start
  6.5 34.0 %cosine_convert_fusion = (bf16[4096,512]{1,0:T(8,128)(2,1)S(1)}, bf16[4096,512]{1,0:T(8,128)(2,1)S(1)}) fusion(s32[512]{0:T(512)S(1)} %iota_add_fusion.1), kind=kLoop, calls=%fused_computation.13 | loop fusion | flops 35651584 | bytes 8390656 | tf_op jit(solution)/shard_map/convert.6
  40.5 0.0 copy-done
  40.5 0.0 copy-start.3
  40.6 1.5 %fusion.17 = f32[64,1024]{1,0:T(8,128)S(1)} fusion(bf16[64,4096]{1,0:T(8,128)(2,1)S(1)} %copy-done, bf16[4096,512]{1,0:T(8,128)(2,1)S(1)} %get-tuple-element.14, bf16[4096,512]{1,0:T(8,128)(2,1)S(1)} %get-tuple-element.13), kind=kOutput, calls=%fused_computation.31 | convolution fusion | flops 553648128 | bytes 9175040 | tf_op jit(solution)/shard_map/dot_general | solution.py:72
  42.1 0.0 copy-start.4
  42.1 0.1 reshape.35
  42.2 0.1 reduce_sum.9
  42.4 0.1 copy.6
  42.5 0.1 copy.7
  42.5 0.1 broadcast_in_dim.11
  42.7 0.1 reshape.36
  42.8 0.0 copy-done.3
  42.9 3.1 %collective-permute-start = (bf16[64,1024]{1,0:T(8,128)(2,1)S(1)}, bf16[64,1024]{1,0:T(8,128)(2,1)S(1)}, u32[]{:S(2)}, u32[]{:S(2)}) collective-permute-start(bf16[64,1024]{1,0:T(8,128)(2,1)S(1)} %pad_maximum_fusion), channel_id=1, source_target_pairs={{0,4},{4,8},{8,12},{12,16},{16,20},{20,24},{24,28},{28,0},{1,5},{5... | collective-permute-start | bytes 393224 | tf_op jit(solution)/shard_map/ppermute | solution.py:15
  45.9 3.1 %collective-permute-start.2 = (bf16[64,1024]{1,0:T(8,128)(2,1)S(1)}, bf16[64,1024]{1,0:T(8,128)(2,1)S(1)}, u32[]{:S(2)}, u32[]{:S(2)}) collective-permute-start(bf16[64,1024]{1,0:T(8,128)(2,1)S(1)} %pad_maximum_fusion), channel_id=1, source_target_pairs={{0,28},{4,0},{8,4},{12,8},{16,12},{20,16},{24,20},{28,24},{1,29},{... | collective-permute-start | bytes 393224 | tf_op jit(solution)/shard_map/ppermute | solution.py:15
  49.0 9.7 %cosine_convert_fusion.1 = (bf16[512,1024]{1,0:T(8,128)(2,1)}, bf16[512,1024]{1,0:T(8,128)(2,1)}) fusion(s32[1024]{0:T(1024)S(1)} %iota_add_fusion, s32[512]{0:T(512)S(1)} %iota_add_fusion.1), kind=kLoop, calls=%fused_computation.30 | loop fusion | flops 8912896 | bytes 2103296 | tf_op jit(solution)/shard_map/convert
  58.8 0.0 collective-permute-done
  58.8 0.0 collective-permute-start.1
  58.8 0.0 copy-done.4
  58.8 0.0 collective-permute-done.2
  58.8 4.8 %collective-permute-start.3 = (bf16[64,1024]{1,0:T(8,128)(2,1)S(1)}, bf16[64,1024]{1,0:T(8,128)(2,1)S(1)}, u32[]{:S(2)}, u32[]{:S(2)}) collective-permute-start(bf16[64,1024]{1,0:T(8,128)(2,1)S(1)} %collective-permute-done.2), channel_id=1, source_target_pairs={{0,28},{4,0},{8,4},{12,8},{16,12},{20,16},{24,20},{28,24},{1,29},{... | collective-permute-start | bytes 393224 | tf_op jit(solution)/shard_map/ppermute | solution.py:15
  63.6 2.9 %collective-permute-done.1 = bf16[64,1024]{1,0:T(8,128)(2,1)S(1)} collective-permute-done((bf16[64,1024]{1,0:T(8,128)(2,1)S(1)}, bf16[64,1024]{1,0:T(8,128)(2,1)S(1)}, u32[]{:S(2)}, u32[]{:S(2)}) %collective-permute-start.1) | collective-permute-done | bytes 131104 | tf_op jit(solution)/shard_map/ppermute | solution.py:15
  66.6 0.1 collective-permute-done.3
  66.7 1.2 %gather_fusion = bf16[256,1024]{1,0:T(8,128)(2,1)S(1)} fusion(bf16[320,1024]{1,0:T(8,128)(2,1)S(1)} %constant_dynamic-update-slice_fusion, s32[1024]{0:T(1024)S(1)} %get-tuple-element.16), kind=kCustom, calls=%fused_computation | custom fusion | bytes 1049600 | tf_op jit(solution)/shard_map/gather | solution.py:89
  67.8 0.1 convert_element_type.17
  68.0 1.2 %gather_fusion.1 = bf16[256,1024]{1,0:T(8,128)(2,1)S(1)} fusion(bf16[320,1024]{1,0:T(8,128)(2,1)S(1)} %constant_dynamic-update-slice_fusion, s32[1024]{0:T(1024)S(1)} %get-tuple-element.15), kind=kCustom, calls=%fused_computation.1 | custom fusion | bytes 1049600 | tf_op jit(solution)/shard_map/gather | solution.py:89
  69.1 0.0 copy-start.1
  69.1 0.0 copy-start.2
  69.1 0.1 convert_element_type.18
  69.3 0.3 add_convert_fusion
  69.5 0.8 copy-done.1
  70.4 0.3 copy-done.2
  70.7 1.7 %fusion.13 = f32[256,1024]{1,0:T(8,128)} fusion(bf16[512,1024]{1,0:T(8,128)(2,1)S(1)} %copy-done.2, bf16[512,1024]{1,0:T(8,128)(2,1)S(1)} %copy-done.1, bf16[256,512]{1,0:T(8,128)(2,1)S(1)} %get-tuple-element.6, bf16[256,512]{1,0:T(8,128)(2,1)S(1)} %get-tuple-element.5), kind=kOutput, calls=%fused_computation.25 | convolution fusion | flops 542113792 | bytes 3670016 | tf_op jit(solution)/shard_map/dot_general | solution.py:93
  72.4 0.0 reduce-scatter.2.cloned.1.call-update
  73.0 25.7 %reduce-scatter.2.cloned.1.call-done = f32[64,1024]{1,0:T(8,128)} async-done(((f32[256,1024]{1,0:T(8,128)}), f32[64,1024]{1,0:T(8,128)}) %reduce-scatter.2.cloned.1.call-update) | async-done | bytes 262160 | tf_op jit(solution)/shard_map/reduce_scatter | solution.py:92
  98.7 1.7 %multiply_select_fusion.1 = f32[64,1024]{1,0:T(8,128)} fusion(f32[64,1024]{1,0:T(8,128)} %reduce-scatter.2.cloned.1.call-done, pred[64]{0:T(512)(128)(4,1)S(1)} %fusion.27), kind=kLoop, calls=%fused_computation.37 | loop fusion | flops 131072 | bytes 524352 | tf_op jit(solution)/shard_map/jit(_where)/select_n | solution.py:103
  (14 shorter events, 0.2 us)
Async XLA Ops:
  6.5 34.0 %copy-start = (bf16[64,4096]{1,0:T(8,128)(2,1)S(1)}, bf16[64,4096]{1,0:T(8,128)(2,1)}, u32[]{:S(2)}) copy-start(bf16[64,4096]{1,0:T(8,128)(2,1)} %param.4) | copy-start | bytes 1572868
  6.5 92.2 %reduce-scatter.2.cloned.1.call-start = ((), (), s32[]{:S(2)}) async-start(), calls=%async_computation.1 | async-start | bytes 1310720 | tf_op jit(solution)/shard_map/reduce_scatter | solution.py:92
  40.5 2.3 %copy-start.3 = (f32[512]{0:T(512)S(1)}, f32[512]{0:T(512)}, u32[]{:S(2)}) copy-start(f32[512]{0:T(512)} %param.5) | copy-start | bytes 6148
  42.1 16.7 %copy-start.4 = (s32[256,2]{0,1:T(2,128)S(1)}, s32[256,2]{0,1:T(2,128)}, u32[]{:S(2)}) copy-start(s32[256,2]{0,1:T(2,128)} %param.6) | copy-start | bytes 6148
  42.9 15.9 %collective-permute-start = (bf16[64,1024]{1,0:T(8,128)(2,1)S(1)}, bf16[64,1024]{1,0:T(8,128)(2,1)S(1)}, u32[]{:S(2)}, u32[]{:S(2)}) collective-permute-start(bf16[64,1024]{1,0:T(8,128)(2,1)S(1)} %pad_maximum_fusion), channel_id=1, source_target_pairs={{0,4},{4,8},{8,12},{12,16},{16,20},{20,24},{24,28},{28,0},{1,5},{5... | collective-permute-start | bytes 393224 | tf_op jit(solution)/shard_map/ppermute | solution.py:15
  45.9 12.9 %collective-permute-start.2 = (bf16[64,1024]{1,0:T(8,128)(2,1)S(1)}, bf16[64,1024]{1,0:T(8,128)(2,1)S(1)}, u32[]{:S(2)}, u32[]{:S(2)}) collective-permute-start(bf16[64,1024]{1,0:T(8,128)(2,1)S(1)} %pad_maximum_fusion), channel_id=1, source_target_pairs={{0,28},{4,0},{8,4},{12,8},{16,12},{20,16},{24,20},{28,24},{1,29},{... | collective-permute-start | bytes 393224 | tf_op jit(solution)/shard_map/ppermute | solution.py:15
  58.8 7.8 %collective-permute-start.1 = (bf16[64,1024]{1,0:T(8,128)(2,1)S(1)}, bf16[64,1024]{1,0:T(8,128)(2,1)S(1)}, u32[]{:S(2)}, u32[]{:S(2)}) collective-permute-start(bf16[64,1024]{1,0:T(8,128)(2,1)S(1)} %collective-permute-done), channel_id=1, source_target_pairs={{0,4},{4,8},{8,12},{12,16},{16,20},{20,24},{24,28},{28,0},{1,5},{5... | collective-permute-start | bytes 393224 | tf_op jit(solution)/shard_map/ppermute | solution.py:15
  58.8 7.8 %collective-permute-start.3 = (bf16[64,1024]{1,0:T(8,128)(2,1)S(1)}, bf16[64,1024]{1,0:T(8,128)(2,1)S(1)}, u32[]{:S(2)}, u32[]{:S(2)}) collective-permute-start(bf16[64,1024]{1,0:T(8,128)(2,1)S(1)} %collective-permute-done.2), channel_id=1, source_target_pairs={{0,28},{4,0},{8,4},{12,8},{16,12},{20,16},{24,20},{28,24},{1,29},{... | collective-permute-start | bytes 393224 | tf_op jit(solution)/shard_map/ppermute | solution.py:15
  69.1 1.2 %copy-start.1 = (bf16[512,1024]{1,0:T(8,128)(2,1)S(1)}, bf16[512,1024]{1,0:T(8,128)(2,1)}, u32[]{:S(2)}) copy-start(bf16[512,1024]{1,0:T(8,128)(2,1)} %get-tuple-element.9) | copy-start | bytes 3145732
  69.1 1.5 %copy-start.2 = (bf16[512,1024]{1,0:T(8,128)(2,1)S(1)}, bf16[512,1024]{1,0:T(8,128)(2,1)}, u32[]{:S(2)}) copy-start(bf16[512,1024]{1,0:T(8,128)(2,1)} %get-tuple-element.10) | copy-start | bytes 3145732
Sparse Core Ops, SparseCore 0:
  72.5 26.1 reduce-scatter.1
where the time goes:
time: 107 us
  other arithmetic  46.2 us (43%)
  waiting for transfers between devices  28.7 us (27%)
  between operations  14.2 us (13%)
  starting transfers between devices  10.9 us (10%)
  local copies, waits for them, and re-layouts  4.04 us (4%)
  matrix products  3.21 us (3%)
    another operation x4, other arithmetic  44 us
    reduce_scatter x1, waiting for transfers between devices, shards(): lax.psum_scatter(jnp.dot(cross, inverse, preferred_element_type=jnp.float...  25.7 us
    ppermute x4, starting transfers between devices, shifted(): return lax.ppermute(value, axis, pairs)  10.9 us
    ppermute x4, waiting for transfers between devices, shifted(): return lax.ppermute(value, axis, pairs)  3 us
    gather x2, local copies, waits for them, and re-layouts, shards(): cross = cross_spectra(local_table[first_row], local_table[second_row])  2.34 us
  transfers between devices with their start and end apart: 5, of which 3 were waited for; matrix products, arithmetic and copies ran while one was open for 9% of the time, Pallas kernels for 0%

commit v1 on v0

v1 whole, which is shorter than its diff:
```python
import functools
import math

import jax
import jax.numpy as jnp
import numpy as np
from jax import lax
from jax.experimental import pallas as pl
from jax.experimental.pallas import tpu as pltpu
from jax.sharding import PartitionSpec as P

NLAG = 1024
BAND = 64
RADIX = 4
LANES = 128
STEP = 64
MESH = pl.DeviceIdType.MESH


def angle_table(rows, cols, period):
    turns = np.mod(np.outer(rows, cols), period).astype(np.float64) * (2.0 * math.pi / period)
    return np.cos(turns), np.sin(turns)


def kernel(
    sizes,
    traces_ref, gain_ref, pairs_ref, limit_ref,
    inner_cos_ref, inner_sin_ref, outer_cos_ref, outer_sin_ref,
    coarse_cos_ref, coarse_sin_ref, fine_cos_ref, fine_sin_ref,
    out_ref,
    table, inverse, part_send, part_recv, sum_send, sum_recv,
    chan_send_sem, chan_recv_sem, pair_send_sem, pair_recv_sem, off_send_sem, off_recv_sem,
):
    chan_total, owners, reach = sizes
    rows, sample_count = traces_ref.shape
    bins = gain_ref.shape[1]
    lags = out_ref.shape[1]
    group = out_ref.shape[0]
    half = owners // 2
    me_chan = lax.axis_index("chan")
    me_off = lax.axis_index("off")
    bin_lo = me_off * bins
    parity = lax.rem(me_off, 2)
    my_half = lax.div(me_off, 2)
    partner = me_off + 1 - 2 * parity

    def chan_peer(shift):
        return lax.rem(me_chan + shift + chan_total, chan_total)

    def off_peer(step):
        return 2 * lax.rem(my_half + step, half) + parity

    shifts = [s for d in range(1, reach + 1) for s in (d, -d)]
    barrier = pltpu.get_barrier_semaphore()
    for shift in shifts:
        pl.semaphore_signal(barrier, inc=1, device_id=(chan_peer(shift), me_off), device_id_type=MESH)
    pl.semaphore_signal(barrier, inc=1, device_id=(me_chan, partner), device_id_type=MESH)
    for step in range(1, half):
        pl.semaphore_signal(barrier, inc=1, device_id=(me_chan, off_peer(step)), device_id_type=MESH)

    inner = sample_count // RADIX
    chunk = RADIX * LANES
    chunks = sample_count // chunk
    odd_half = lax.rem(lax.div(bin_lo, inner // 2), 2)
    src = lax.broadcasted_iota(jnp.int32, (chunk, chunk), 0)
    dst = lax.broadcasted_iota(jnp.int32, (chunk, chunk), 1)
    lane = lax.rem(dst, LANES)
    wanted = RADIX * lane + lax.div(dst, LANES)
    flip = 1.0 - 2.0 * (lax.rem(lane, 2) * odd_half).astype(jnp.float32)
    spread = jnp.where(src == wanted, flip, 0.0).astype(jnp.bfloat16)
    stacked = jnp.concatenate([traces_ref[:, c * chunk:(c + 1) * chunk] for c in range(chunks)], axis=0)
    split = jnp.dot(stacked, spread, preferred_element_type=jnp.float32).astype(jnp.bfloat16)
    by_residue = jnp.concatenate(
        [
            jnp.concatenate(
                [split[c * rows:(c + 1) * rows, r * LANES:(r + 1) * LANES] for c in range(chunks)], axis=1
            )
            for r in range(RADIX)
        ],
        axis=0,
    )
    col_lo = pl.multiple_of(lax.rem(bin_lo, inner // 2), LANES)
    in_re = jnp.dot(by_residue, inner_cos_ref[:, pl.ds(col_lo, bins)], preferred_element_type=jnp.float32)
    in_im = jnp.dot(by_residue, inner_sin_ref[:, pl.ds(col_lo, bins)], preferred_element_type=jnp.float32)
    tw_lo = pl.multiple_of(bin_lo, LANES)
    real_part = in_re[:rows]
    imag_part = in_im[:rows]
    for r in range(1, RADIX):
        tc = outer_cos_ref[r:r + 1, pl.ds(tw_lo, bins)]
        ts = outer_sin_ref[r:r + 1, pl.ds(tw_lo, bins)]
        a = in_re[r * rows:(r + 1) * rows]
        b = in_im[r * rows:(r + 1) * rows]
        real_part += a * tc - b * ts
        imag_part += a * ts + b * tc

    power = real_part * real_part + imag_part * imag_part
    high = power.astype(jnp.bfloat16)
    low = (power - high.astype(jnp.float32)).astype(jnp.bfloat16)
    band_a = lax.div(lax.broadcasted_iota(jnp.int32, (bins, bins), 0), BAND)
    band_b = lax.div(lax.broadcasted_iota(jnp.int32, (bins, bins), 1), BAND)
    mean_of = jnp.where(band_a == band_b, 1.0 / BAND, 0.0).astype(jnp.bfloat16)
    mean = jnp.dot(high, mean_of, preferred_element_type=jnp.float32) + jnp.dot(
        low, mean_of, preferred_element_type=jnp.float32
    )
    scale = lax.rsqrt(mean + 1e-06) * gain_ref[...]
    own = table.at[reach]
    own[:, :bins] = (real_part * scale).astype(jnp.bfloat16)
    own[:, bins:] = (imag_part * scale).astype(jnp.bfloat16)

    pl.semaphore_wait(barrier, len(shifts) + half)

    moves = []
    for i, shift in enumerate(shifts):
        moves.append(
            pltpu.make_async_remote_copy(
                src_ref=own,
                dst_ref=table.at[reach - shift],
                send_sem=chan_send_sem.at[i],
                recv_sem=chan_recv_sem.at[i],
                device_id=(chan_peer(shift), me_off),
                device_id_type=MESH,
            )
        )
    for move in reversed(moves):
        move.start()

    row_lo = lax.div(bin_lo, STEP)

    def fill(a, carry):
        cc = coarse_cos_ref[pl.ds(row_lo + a, 1), :]
        cs = coarse_sin_ref[pl.ds(row_lo + a, 1), :]
        fc = fine_cos_ref[...]
        fs = fine_sin_ref[...]
        at = pl.multiple_of(a * STEP, STEP)
        inverse[pl.ds(at, STEP), :] = (cc * fc - cs * fs).astype(jnp.bfloat16)
        inverse[pl.ds(bins + at, STEP), :] = (-(cs * fc + cc * fs)).astype(jnp.bfloat16)
        return carry

    lax.fori_loop(0, bins // STEP, fill, 0)

    for move in moves:
        move.wait_recv()

    span = (2 * reach + 1) * rows
    chan_a = me_chan * rows + lax.broadcasted_iota(jnp.int32, (1, rows), 1)
    chan_b = (me_chan - reach) * rows + lax.broadcasted_iota(jnp.int32, (1, span), 1)
    chan_b = jnp.where(chan_b < 0, chan_b + chan_total * rows, chan_b)
    chan_b = jnp.where(chan_b >= chan_total * rows, chan_b - chan_total * rows, chan_b)

    def lag_rows(par):
        pairs = jnp.concatenate(
            [pairs_ref[pl.ds(pl.multiple_of((2 * h + par) * group, group), group), :] for h in range(half)], axis=0
        )
        pick_a = jnp.where(pairs[:, 0:1] == chan_a, 1.0, 0.0).astype(jnp.bfloat16)
        pick_b = jnp.where(pairs[:, 1:2] == chan_b, 1.0, 0.0).astype(jnp.bfloat16)
        left = jnp.dot(pick_a, own[...], preferred_element_type=jnp.float32)
        right = jnp.dot(
            pick_b, table[...].reshape(span, 2 * bins), preferred_element_type=jnp.float32
        )
        la, lb = left[:, :bins], left[:, bins:]
        ra, rb = right[:, :bins], right[:, bins:]
        cross = jnp.concatenate([la * ra + lb * rb, la * rb - lb * ra], axis=1).astype(jnp.bfloat16)
        return jnp.dot(cross, inverse[...], preferred_element_type=jnp.float32)

    part_send[...] = lag_rows(1 - parity).astype(part_send.dtype)
    swap = pltpu.make_async_remote_copy(
        src_ref=part_send,
        dst_ref=part_recv,
        send_sem=pair_send_sem,
        recv_sem=pair_recv_sem,
        device_id=(me_chan, partner),
        device_id_type=MESH,
    )
    swap.start()
    mine = lag_rows(parity)
    swap.wait_recv()
    mine = mine + part_recv[...].astype(jnp.float32)
    for h in range(half):
        sum_send[h] = mine[h * group:(h + 1) * group]
    narrow = sum_recv.dtype
    sends = []
    for step in range(1, half):
        slot = lax.rem(my_half + step, half)
        part_send_slot = sum_send.at[slot]
        sends.append(part_send_slot)
    out_ref[...] = sum_send[my_half]
    moves_off = []
    stage = part_recv
    for step in range(1, half):
        slot = lax.rem(my_half + step, half)
        stage[pl.ds((step - 1) * group, group), :] = sum_send[slot].astype(narrow)
        moves_off.append(
            pltpu.make_async_remote_copy(
                src_ref=stage.at[pl.ds((step - 1) * group, group), :],
                dst_ref=sum_recv.at[step - 1],
                send_sem=off_send_sem.at[step - 1],
                recv_sem=off_recv_sem.at[step - 1],
                device_id=(me_chan, off_peer(step)),
                device_id_type=MESH,
            )
        )
        moves_off[-1].start()
    total = out_ref[...]
    for step in range(1, half):
        moves_off[step - 1].wait_recv()
        total = total + sum_recv[step - 1].astype(jnp.float32)
    live = lax.broadcasted_iota(jnp.int32, (group, 1), 0) < limit_ref[0]
    out_ref[...] = jnp.where(live, total * (1.0 / math.sqrt(sample_count // 2)), 0.0)
    for move in moves:
        move.wait_send()
    swap.wait_send()
    for move in moves_off:
        move.wait_send()


def shards(traces, band_gain, pair_list, pair_count):
    chan_total = lax.axis_size("chan")
    owners = lax.axis_size("off")
    reach = chan_total // 4
    rows, sample_count = traces.shape
    bins = band_gain.shape[0]
    group = pair_list.shape[0] // owners
    half = owners // 2
    inner = sample_count // RADIX
    all_bins = bins * owners
    assert (inner // 2) % bins == 0 and bins % STEP == 0

    def const(value, dtype):
        return jnp.asarray(value, dtype=dtype)

    ic, isn = angle_table(np.arange(inner), np.arange(inner // 2), inner)
    oc, osn = angle_table(np.arange(RADIX), np.arange(all_bins), sample_count)
    lag_ids = np.arange(NLAG) - NLAG // 2
    cc, cs = angle_table(np.arange(0, all_bins, STEP), lag_ids, sample_count)
    fc, fs = angle_table(np.arange(STEP), lag_ids, sample_count)
    vmem = pl.BlockSpec(memory_space=pltpu.VMEM)
    smem = pl.BlockSpec(memory_space=pltpu.SMEM)
    dma = pltpu.SemaphoreType.DMA
    peers = max(1, half - 1)
    return pl.pallas_call(
        functools.partial(kernel, (chan_total, owners, reach)),
        out_shape=jax.ShapeDtypeStruct((group, NLAG), jnp.float32),
        in_specs=[vmem, vmem, vmem, smem] + [vmem] * 8,
        out_specs=vmem,
        scratch_shapes=[
            pltpu.VMEM((2 * reach + 1, rows, 2 * bins), jnp.bfloat16),
            pltpu.VMEM((2 * bins, NLAG), jnp.bfloat16),
            pltpu.VMEM((half * group, NLAG), jnp.bfloat16),
            pltpu.VMEM((half * group, NLAG), jnp.bfloat16),
            pltpu.VMEM((half, group, NLAG), jnp.float32),
            pltpu.VMEM((peers, group, NLAG), jnp.bfloat16),
            dma((2 * reach,)), dma((2 * reach,)),
            dma, dma,
            dma((peers,)), dma((peers,)),
        ],
        compiler_params=pltpu.CompilerParams(
            collective_id=0, has_side_effects=True, vmem_limit_bytes=48 * 1024 * 1024
        ),
        name="correlate",
    )(
        traces, band_gain.reshape(1, bins), pair_list, pair_count,
        const(ic, jnp.bfloat16), const(-isn, jnp.bfloat16),
        const(oc, jnp.float32), const(-osn, jnp.float32),
        const(cc, jnp.float32), const(cs, jnp.float32),
        const(fc, jnp.float32), const(fs, jnp.float32),
    )


def solution(mesh):
    placed = (P("chan", None), P("off"), P("chan", None), P(("chan", "off")))
    return jax.shard_map(
        shards, mesh=mesh, in_specs=placed, out_specs=P(("chan", "off"), None), check_vma=False
    )
```

time: 107 us -> 34.6 us (0.32)
  other arithmetic: 46.2 us -> 0 us
  waiting for transfers between devices: 28.7 us -> 0 us
  Pallas kernels: 0 us -> 24.1 us
  between operations: 14.2 us -> 0.74 us
  starting transfers between devices: 10.9 us -> 0 us
  local copies, waits for them, and re-layouts: 4.04 us -> 9.33 us
  matrix products: 3.21 us -> 0 us
    another operation x4 -> x0, other arithmetic: 44 us -> none
    reduce_scatter x1 -> x0, waiting for transfers between devices: 25.7 us -> none  [shards(): lax.psum_scatter(jnp.dot(cross, inverse, preferred_element_type=jnp.float...]
    pallas_call x0 -> x1, Pallas kernels: none -> 24.1 us  [shards(): pl.pallas_call(functools.partial(kernel, (chan_total, owners, reach)), ou...]
    ppermute x4 -> x0, starting transfers between devices: 10.9 us -> none  [shifted(): return lax.ppermute(value, axis, pairs)]
    unnamed x13 -> x22, local copies, waits for them, and re-layouts: 1.19 us -> 9.33 us
    dot_general x2 -> x0, matrix products: 3.21 us -> none  [the longest x1 1.68 us: shards(): jnp.dot(cross, inverse, preferred_element_type=jnp.float32)]
    ppermute x4 -> x0, waiting for transfers between devices: 3 us -> none  [shifted(): return lax.ppermute(value, axis, pairs)]
    gather x2 -> x0, local copies, waits for them, and re-layouts: 2.34 us -> none  [shards(): cross = cross_spectra(local_table[first_row], local_table[second_row])]
  transfers between devices with their start and end apart: 5 -> 0, of which waited for: 3 -> 0; matrix products, arithmetic and copies ran while one was open for 9% -> 0% of each run, Pallas kernels for 0% -> 0%
where the time goes in v1:
time: 34.6 us; the launch traced here: 34.1 us
  Pallas kernels  24.1 us (70%)
  local copies, waits for them, and re-layouts  9.33 us (27%)
  between operations  0.74 us (2%)
    pallas_call x1, Pallas kernels, shards(): pl.pallas_call(functools.partial(kernel, (chan_total, owners, reach)), ou...  24.1 us
    unnamed x22, local copies, waits for them, and re-layouts  9.33 us

profile of v1, /device:TPU:0, one launch (start us, length us, event | category | flops | bytes accessed | tf_op | source)
XLA Modules:
  0.0 34.1 jit_solution(14349086890675413171)
XLA Ops:
  0.0 0.0 copy-start.5
  0.7 0.0 copy-start.9
  0.7 0.8 %copy.13.pairs_ref = s32[256,2]{1,0:T(8,128)S(1)} copy(s32[256,2]{0,1:T(2,128)} %param.14) | data formatting | bytes 4096 | tf_op args[2]
  1.5 0.0 copy-done.5
  1.5 0.0 copy-done.9
  1.5 0.0 copy-start
  1.6 1.2 %copy-done = bf16[1024,512]{1,0:T(8,128)(2,1)S(1)} copy-done((bf16[1024,512]{1,0:T(8,128)(2,1)S(1)}, bf16[1024,512]{1,0:T(8,128)(2,1)}, u32[]{:S(2)}) %copy-start) | copy-done | bytes 1048600
  2.8 0.0 copy-start.1
  2.8 1.2 %copy-done.1 = bf16[1024,512]{1,0:T(8,128)(2,1)S(1)} copy-done((bf16[1024,512]{1,0:T(8,128)(2,1)S(1)}, bf16[1024,512]{1,0:T(8,128)(2,1)}, u32[]{:S(2)}) %copy-start.1) | copy-done | bytes 1048600
  4.0 0.0 copy-start.2
  4.0 1.0 %copy-done.2 = bf16[64,4096]{1,0:T(8,128)(2,1)S(1)} copy-done((bf16[64,4096]{1,0:T(8,128)(2,1)S(1)}, bf16[64,4096]{1,0:T(8,128)(2,1)}, u32[]{:S(2)}) %copy-start.2) | copy-done | bytes 524312
  5.0 0.0 copy-start.3
  5.0 0.9 %copy-done.3 = f32[64,1024]{1,0:T(8,128)S(1)} copy-done((f32[64,1024]{1,0:T(8,128)S(1)}, f32[64,1024]{1,0:T(8,128)}, u32[]{:S(2)}) %copy-start.3) | copy-done | bytes 262168
  6.0 0.0 copy-start.4
  6.0 0.9 %copy-done.4 = f32[64,1024]{1,0:T(8,128)S(1)} copy-done((f32[64,1024]{1,0:T(8,128)S(1)}, f32[64,1024]{1,0:T(8,128)}, u32[]{:S(2)}) %copy-start.4) | copy-done | bytes 262168
  6.9 0.0 copy-start.6
  6.9 0.9 %copy-done.6 = f32[32,1024]{1,0:T(8,128)S(1)} copy-done((f32[32,1024]{1,0:T(8,128)S(1)}, f32[32,1024]{1,0:T(8,128)}, u32[]{:S(2)}) %copy-start.6) | copy-done | bytes 131096
  7.8 0.0 copy-start.7
  7.8 0.8 %copy-done.7 = f32[4,2048]{1,0:T(4,128)S(1)} copy-done((f32[4,2048]{1,0:T(4,128)S(1)}, f32[4,2048]{1,0:T(4,128)}, u32[]{:S(2)}) %copy-start.7) | copy-done | bytes 32792
  8.6 0.0 copy-start.8
  8.6 0.8 %copy-done.8 = f32[4,2048]{1,0:T(4,128)S(1)} copy-done((f32[4,2048]{1,0:T(4,128)S(1)}, f32[4,2048]{1,0:T(4,128)}, u32[]{:S(2)}) %copy-start.8) | copy-done | bytes 32792
  9.4 24.1 %correlate.1 = f32[64,1024]{1,0:T(8,128)S(1)} custom-call(bf16[64,4096]{1,0:T(8,128)(2,1)S(1)} %copy-done.2, f32[1,512]{1,0:T(1,128)S(1)} %bitcast.1, s32[256,2]{1,0:T(8,128)S(1)} %copy.13.pairs_ref, s32[1]{0:T(128)S(6)} %copy.15.limit_ref, bf16[1024,512]{1,0:T(8,128)(2,1)S(1)} %copy-done.1, bf16[1024,512]{1,0:T(8,128)(2,1)S(1)} %copy-done, ...), custom_call_target="tpu_custom_call" | custom-call | tf_op jit(solution)/shard_map/correlate/pallas_call | solution.py:240
  33.4 0.7 %copy.16 = f32[64,1024]{1,0:T(8,128)} copy(f32[64,1024]{1,0:T(8,128)S(1)} %correlate.1) | data formatting | bytes 524288
Async XLA Ops:
  0.0 1.5 %copy-start.5 = (f32[32,1024]{1,0:T(8,128)S(1)}, f32[32,1024]{1,0:T(8,128)}, u32[]{:S(2)}) copy-start(f32[32,1024]{1,0:T(8,128)} %constant.21.clone.coarse_sin_ref) | copy-start | bytes 393220
  0.7 0.8 %copy-start.9 = (f32[512]{0:T(512)S(1)}, f32[512]{0:T(512)}, u32[]{:S(2)}) copy-start(f32[512]{0:T(512)} %param.13) | copy-start | bytes 6148
  1.5 1.2 %copy-start = (bf16[1024,512]{1,0:T(8,128)(2,1)S(1)}, bf16[1024,512]{1,0:T(8,128)(2,1)}, u32[]{:S(2)}) copy-start(bf16[1024,512]{1,0:T(8,128)(2,1)} %constant.17.clone.inner_sin_ref) | copy-start | bytes 3145732
  2.8 1.2 %copy-start.1 = (bf16[1024,512]{1,0:T(8,128)(2,1)S(1)}, bf16[1024,512]{1,0:T(8,128)(2,1)}, u32[]{:S(2)}) copy-start(bf16[1024,512]{1,0:T(8,128)(2,1)} %constant.16.clone.inner_cos_ref) | copy-start | bytes 3145732
  4.0 1.0 %copy-start.2 = (bf16[64,4096]{1,0:T(8,128)(2,1)S(1)}, bf16[64,4096]{1,0:T(8,128)(2,1)}, u32[]{:S(2)}) copy-start(bf16[64,4096]{1,0:T(8,128)(2,1)} %traces_ref.1) | copy-start | bytes 1572868
  5.0 0.9 %copy-start.3 = (f32[64,1024]{1,0:T(8,128)S(1)}, f32[64,1024]{1,0:T(8,128)}, u32[]{:S(2)}) copy-start(f32[64,1024]{1,0:T(8,128)} %constant.23.clone.fine_sin_ref) | copy-start | bytes 786436
  6.0 0.9 %copy-start.4 = (f32[64,1024]{1,0:T(8,128)S(1)}, f32[64,1024]{1,0:T(8,128)}, u32[]{:S(2)}) copy-start(f32[64,1024]{1,0:T(8,128)} %constant.22.clone.fine_cos_ref) | copy-start | bytes 786436
  6.9 0.9 %copy-start.6 = (f32[32,1024]{1,0:T(8,128)S(1)}, f32[32,1024]{1,0:T(8,128)}, u32[]{:S(2)}) copy-start(f32[32,1024]{1,0:T(8,128)} %constant.20.clone.coarse_cos_ref) | copy-start | bytes 393220
  7.8 0.8 %copy-start.7 = (f32[4,2048]{1,0:T(4,128)S(1)}, f32[4,2048]{1,0:T(4,128)}, u32[]{:S(2)}) copy-start(f32[4,2048]{1,0:T(4,128)} %constant.19.clone.outer_sin_ref) | copy-start | bytes 98308
  8.6 0.8 %copy-start.8 = (f32[4,2048]{1,0:T(4,128)S(1)}, f32[4,2048]{1,0:T(4,128)}, u32[]{:S(2)}) copy-start(f32[4,2048]{1,0:T(4,128)} %constant.18.clone.outer_cos_ref) | copy-start | bytes 98308

commit v2 on v1

--- a/solution.py
+++ b/solution.py
@@ -24,10 +24,9 @@
 
 def kernel(
     sizes,
-    traces_ref, gain_ref, pairs_ref, limit_ref,
-    inner_cos_ref, inner_sin_ref, outer_cos_ref, outer_sin_ref,
-    coarse_cos_ref, coarse_sin_ref, fine_cos_ref, fine_sin_ref,
+    traces_hbm, gain_hbm, pairs_hbm, limit_hbm, inner_hbm, outer_hbm, coarse_hbm, fine_hbm,
     out_ref,
+    traces_ref, gain_ref, pairs_ref, limit_ref, inner_ref, outer_ref, coarse_ref, fine_ref, slots, load_sem,
     table, inverse, part_send, part_recv, sum_send, sum_recv,
     chan_send_sem, chan_recv_sem, pair_send_sem, pair_recv_sem, off_send_sem, off_recv_sem,
 ):
@@ -50,6 +49,18 @@
     def off_peer(step):
         return 2 * lax.rem(my_half + step, half) + parity
 
+    loads = [
+        pltpu.make_async_copy(source, target, load_sem.at[i])
+        for i, (source, target) in enumerate(
+            (
+                (traces_hbm, traces_ref), (inner_hbm, inner_ref), (outer_hbm, outer_ref), (gain_hbm, gain_ref),
+                (fine_hbm, fine_ref), (coarse_hbm, coarse_ref), (pairs_hbm, pairs_ref), (limit_hbm, limit_ref),
+            )
+        )
+    ]
+    for load in loads:
+        load.start()
+
     shifts = [s for d in range(1, reach + 1) for s in (d, -d)]
     barrier = pltpu.get_barrier_semaphore()
     for shift in shifts:
@@ -68,6 +79,7 @@
     wanted = RADIX * lane + lax.div(dst, LANES)
     flip = 1.0 - 2.0 * (lax.rem(lane, 2) * odd_half).astype(jnp.float32)
     spread = jnp.where(src == wanted, flip, 0.0).astype(jnp.bfloat16)
+    loads[0].wait()
     stacked = jnp.concatenate([traces_ref[:, c * chunk:(c + 1) * chunk] for c in range(chunks)], axis=0)
     split = jnp.dot(stacked, spread, preferred_element_type=jnp.float32).astype(jnp.bfloat16)
     by_residue = jnp.concatenate(
@@ -80,14 +92,17 @@
         axis=0,
     )
     col_lo = pl.multiple_of(lax.rem(bin_lo, inner // 2), LANES)
-    in_re = jnp.dot(by_residue, inner_cos_ref[:, pl.ds(col_lo, bins)], preferred_element_type=jnp.float32)
-    in_im = jnp.dot(by_residue, inner_sin_ref[:, pl.ds(col_lo, bins)], preferred_element_type=jnp.float32)
+    loads[1].wait()
+    in_re = jnp.dot(by_residue, inner_ref[0, :, pl.ds(col_lo, bins)], preferred_element_type=jnp.float32)
+    in_im = jnp.dot(by_residue, inner_ref[1, :, pl.ds(col_lo, bins)], preferred_element_type=jnp.float32)
     tw_lo = pl.multiple_of(bin_lo, LANES)
+    loads[2].wait()
+    loads[3].wait()
     real_part = in_re[:rows]
     imag_part = in_im[:rows]
     for r in range(1, RADIX):
-        tc = outer_cos_ref[r:r + 1, pl.ds(tw_lo, bins)]
-        ts = outer_sin_ref[r:r + 1, pl.ds(tw_lo, bins)]
+        tc = outer_ref[r:r + 1, pl.ds(tw_lo, bins)]
+        ts = outer_ref[RADIX + r:RADIX + r + 1, pl.ds(tw_lo, bins)]
         a = in_re[r * rows:(r + 1) * rows]
         b = in_im[r * rows:(r + 1) * rows]
         real_part += a * tc - b * ts
@@ -124,13 +139,16 @@
     for move in reversed(moves):
         move.start()
 
+    for load in loads[4:]:
+        load.wait()
+    slots[...] = jnp.transpose(pairs_ref[...])
     row_lo = lax.div(bin_lo, STEP)
 
     def fill(a, carry):
-        cc = coarse_cos_ref[pl.ds(row_lo + a, 1), :]
-        cs = coarse_sin_ref[pl.ds(row_lo + a, 1), :]
-        fc = fine_cos_ref[...]
-        fs = fine_sin_ref[...]
+        cc = coarse_ref[0, pl.ds(row_lo + a, 1), :]
+        cs = coarse_ref[1, pl.ds(row_lo + a, 1), :]
+        fc = fine_ref[0]
+        fs = fine_ref[1]
         at = pl.multiple_of(a * STEP, STEP)
         inverse[pl.ds(at, STEP), :] = (cc * fc - cs * fs).astype(jnp.bfloat16)
         inverse[pl.ds(bins + at, STEP), :] = (-(cs * fc + cc * fs)).astype(jnp.bfloat16)
@@ -149,7 +167,7 @@
 
     def lag_rows(par):
         pairs = jnp.concatenate(
-            [pairs_ref[pl.ds(pl.multiple_of((2 * h + par) * group, group), group), :] for h in range(half)], axis=0
+            [slots[pl.ds(pl.multiple_of((2 * h + par) * group, group), group), :] for h in range(half)], axis=0
         )
         pick_a = jnp.where(pairs[:, 0:1] == chan_a, 1.0, 0.0).astype(jnp.bfloat16)
         pick_b = jnp.where(pairs[:, 1:2] == chan_b, 1.0, 0.0).astype(jnp.bfloat16)
@@ -234,15 +252,24 @@
     cc, cs = angle_table(np.arange(0, all_bins, STEP), lag_ids, sample_count)
     fc, fs = angle_table(np.arange(STEP), lag_ids, sample_count)
     vmem = pl.BlockSpec(memory_space=pltpu.VMEM)
-    smem = pl.BlockSpec(memory_space=pltpu.SMEM)
+    hbm = pl.BlockSpec(memory_space=pltpu.HBM)
     dma = pltpu.SemaphoreType.DMA
     peers = max(1, half - 1)
+    operands = (
+        traces, band_gain.reshape(1, bins), pair_list.T, pair_count,
+        const(np.stack([ic, -isn]), jnp.bfloat16),
+        const(np.concatenate([oc, -osn]), jnp.float32),
+        const(np.stack([cc, cs]), jnp.float32),
+        const(np.stack([fc, fs]), jnp.float32),
+    )
     return pl.pallas_call(
         functools.partial(kernel, (chan_total, owners, reach)),
         out_shape=jax.ShapeDtypeStruct((group, NLAG), jnp.float32),
-        in_specs=[vmem, vmem, vmem, smem] + [vmem] * 8,
+        in_specs=[hbm] * 8,
         out_specs=vmem,
         scratch_shapes=[
+            *[(pltpu.SMEM if x.shape == (1,) else pltpu.VMEM)(x.shape, x.dtype) for x in operands],
+            pltpu.VMEM(pair_list.shape, jnp.int32), dma((len(operands),)),
             pltpu.VMEM((2 * reach + 1, rows, 2 * bins), jnp.bfloat16),
             pltpu.VMEM((2 * bins, NLAG), jnp.bfloat16),
             pltpu.VMEM((half * group, NLAG), jnp.bfloat16),
@@ -254,16 +281,10 @@
             dma((peers,)), dma((peers,)),
         ],
         compiler_params=pltpu.CompilerParams(
-            collective_id=0, has_side_effects=True, vmem_limit_bytes=48 * 1024 * 1024
+            collective_id=0, has_side_effects=True, vmem_limit_bytes=60 * 1024 * 1024
         ),
         name="correlate",
-    )(
-        traces, band_gain.reshape(1, bins), pair_list, pair_count,
-        const(ic, jnp.bfloat16), const(-isn, jnp.bfloat16),
-        const(oc, jnp.float32), const(-osn, jnp.float32),
-        const(cc, jnp.float32), const(cs, jnp.float32),
-        const(fc, jnp.float32), const(fs, jnp.float32),
-    )
+    )(*operands)
 
 
 def solution(mesh):

time: 34.6 us -> 28.8 us (0.83)
  local copies, waits for them, and re-layouts: 9.33 us -> 1.67 us
  Pallas kernels: 24.1 us -> 26.3 us
    unnamed x22 -> x1, local copies, waits for them, and re-layouts: 9.33 us -> 1.67 us
    pallas_call x1, Pallas kernels: 24.1 us -> 26.3 us  [shards(): pl.pallas_call(functools.partial(kernel, (chan_total, owners, reach)), ou...]
where the time goes in v2:
time: 28.8 us; the launch traced here: 28.7 us
  Pallas kernels  26.3 us (91%)
  local copies, waits for them, and re-layouts  1.67 us (6%)
  between operations  0.66 us (2%)
    pallas_call x1, Pallas kernels, shards(): pl.pallas_call(functools.partial(kernel, (chan_total, owners, reach)), ou...  26.3 us
    unnamed x1, local copies, waits for them, and re-layouts  1.67 us

profile of v2, /device:TPU:0, one launch (start us, length us, event | category | flops | bytes accessed | tf_op | source)
XLA Modules:
  0.0 28.7 jit_solution(6281569308318713395)
XLA Ops:
  0.7 26.3 %correlate.1 = f32[64,1024]{1,0:T(8,128)} custom-call(bf16[64,4096]{1,0:T(8,128)(2,1)} %traces_hbm.1, f32[1,512]{1,0:T(1,128)} %bitcast.2, s32[2,256]{1,0:T(2,128)} %bitcast.3, s32[1]{0:T(128)S(6)} %copy.10.limit_hbm, bf16[2,1024,512]{2,1,0:T(8,128)(2,1)} %constant.8.clone.inner_hbm, f32[8,2048]{1,0:T(8,128)} %constant.9.clone.outer_hbm, ...), custom_call_target="tpu_custom_call" | custom-call | tf_op jit(solution)/shard_map/correlate/pallas_call | solution.py:265
  27.0 1.7 %copy.11 = f32[64,1024]{1,0:T(8,128)} copy(f32[64,1024]{1,0:T(8,128)} %correlate.1) | data formatting | bytes 524288

commit v3 on v2

v3 whole, which is shorter than its diff:
```python
import functools
import math

import jax
import jax.numpy as jnp
import numpy as np
from jax import lax
from jax.experimental import pallas as pl
from jax.experimental.pallas import tpu as pltpu
from jax.sharding import PartitionSpec as P

NLAG = 1024
BAND = 64
RADIX = 4
LANES = 128
STEP = 64
MESH = pl.DeviceIdType.MESH


def angle_table(rows, cols, period):
    turns = np.mod(np.outer(rows, cols), period).astype(np.float64) * (2.0 * math.pi / period)
    return np.cos(turns), np.sin(turns)


def kernel(
    sizes,
    traces_hbm, gain_hbm, pairs_hbm, inner_hbm, outer_hbm, coarse_hbm, fine_hbm,
    out_ref,
    traces_ref, gain_ref, pairs_ref, inner_ref, outer_ref, coarse_ref, fine_ref, slots, load_sem,
    table, inverse, total, swap_send, swap_recv, sum_send, sum_recv,
    chan_send_sem, chan_recv_sem, swap_send_sem, swap_recv_sem, off_send_sem, off_recv_sem,
):
    chan_total, owners, reach = sizes
    rows, sample_count = traces_ref.shape
    bins = gain_ref.shape[1]
    group = out_ref.shape[0]
    half = owners // 2
    pieces = bins // LANES
    me_chan = lax.axis_index("chan")
    me_off = lax.axis_index("off")
    bin_lo = me_off * bins
    parity = lax.rem(me_off, 2)
    my_half = lax.div(me_off, 2)
    partner = me_off + 1 - 2 * parity

    def chan_peer(shift):
        return lax.rem(me_chan + shift + chan_total, chan_total)

    def off_peer(step):
        return 2 * lax.rem(my_half + step, half) + parity

    loads = [
        pltpu.make_async_copy(source, target, load_sem.at[i])
        for i, (source, target) in enumerate(
            (
                (traces_hbm, traces_ref), (inner_hbm, inner_ref), (outer_hbm, outer_ref), (gain_hbm, gain_ref),
                (fine_hbm, fine_ref), (coarse_hbm, coarse_ref), (pairs_hbm, pairs_ref),
            )
        )
    ]
    for load in loads:
        load.start()

    shifts = [s for d in range(reach, 0, -1) for s in (d, -d)]
    barrier = pltpu.get_barrier_semaphore()
    for shift in shifts:
        pl.semaphore_signal(barrier, inc=1, device_id=(chan_peer(shift), me_off), device_id_type=MESH)
    pl.semaphore_signal(barrier, inc=1, device_id=(me_chan, partner), device_id_type=MESH)
    for step in range(1, half):
        pl.semaphore_signal(barrier, inc=1, device_id=(me_chan, off_peer(step)), device_id_type=MESH)

    inner = sample_count // RADIX
    chunk = RADIX * LANES
    chunks = sample_count // chunk
    odd_half = lax.rem(lax.div(bin_lo, inner // 2), 2)
    src = lax.broadcasted_iota(jnp.int32, (chunk, chunk), 0)
    dst = lax.broadcasted_iota(jnp.int32, (chunk, chunk), 1)
    lane = lax.rem(dst, LANES)
    wanted = RADIX * lane + lax.div(dst, LANES)
    flip = 1.0 - 2.0 * (lax.rem(lane, 2) * odd_half).astype(jnp.float32)
    spread = jnp.where(src == wanted, flip, 0.0).astype(jnp.bfloat16)
    band_a = lax.div(lax.broadcasted_iota(jnp.int32, (LANES, LANES), 0), BAND)
    band_b = lax.div(lax.broadcasted_iota(jnp.int32, (LANES, LANES), 1), BAND)
    mean_of = jnp.where(band_a == band_b, 1.0 / BAND, 0.0).astype(jnp.bfloat16)
    loads[0].wait()
    stacked = jnp.concatenate([traces_ref[:, c * chunk:(c + 1) * chunk] for c in range(chunks)], axis=0)
    split = jnp.dot(stacked, spread, preferred_element_type=jnp.float32).astype(jnp.bfloat16)
    by_residue = jnp.concatenate(
        [
            jnp.concatenate(
                [split[c * rows:(c + 1) * rows, r * LANES:(r + 1) * LANES] for c in range(chunks)], axis=1
            )
            for r in range(RADIX)
        ],
        axis=0,
    )
    for load in loads[1:4]:
        load.wait()
    col_lo = lax.rem(bin_lo, inner // 2)

    moves = []
    for q in range(pieces):
        at = pl.multiple_of(2 * (col_lo + q * LANES), LANES)
        part = jnp.dot(by_residue, inner_ref[:, pl.ds(at, 2 * LANES)], preferred_element_type=jnp.float32)
        real_part = part[:rows, :LANES]
        imag_part = part[:rows, LANES:]
        tw = pl.ds(pl.multiple_of(bin_lo + q * LANES, LANES), LANES)
        for r in range(1, RADIX):
            tc = outer_ref[r:r + 1, tw]
            ts = outer_ref[RADIX + r:RADIX + r + 1, tw]
            a = part[r * rows:(r + 1) * rows, :LANES]
            b = part[r * rows:(r + 1) * rows, LANES:]
            real_part += a * tc - b * ts
            imag_part += a * ts + b * tc
        power = real_part * real_part + imag_part * imag_part
        high = power.astype(jnp.bfloat16)
        low = (power - high.astype(jnp.float32)).astype(jnp.bfloat16)
        mean = jnp.dot(high, mean_of, preferred_element_type=jnp.float32) + jnp.dot(
            low, mean_of, preferred_element_type=jnp.float32
        )
        scale = lax.rsqrt(mean + 1e-06) * gain_ref[:, q * LANES:(q + 1) * LANES]
        table[q, reach, :, :LANES] = (real_part * scale).astype(jnp.bfloat16)
        table[q, reach, :, LANES:] = (imag_part * scale).astype(jnp.bfloat16)
        if q == 0:
            pl.semaphore_wait(barrier, len(shifts) + half)
        for i, shift in enumerate(shifts):
            move = pltpu.make_async_remote_copy(
                src_ref=table.at[q, reach],
                dst_ref=table.at[q, reach - shift],
                send_sem=chan_send_sem.at[q, i],
                recv_sem=chan_recv_sem.at[q, i],
                device_id=(chan_peer(shift), me_off),
                device_id_type=MESH,
            )
            move.start()
            moves.append(move)

    for load in loads[4:]:
        load.wait()
    slots[...] = jnp.transpose(pairs_ref[...])
    row_lo = lax.div(bin_lo, STEP)
    per = LANES // STEP

    def fill(a, carry):
        cc = coarse_ref[0, pl.ds(row_lo + a, 1), :]
        cs = coarse_ref[1, pl.ds(row_lo + a, 1), :]
        fc = fine_ref[0]
        fs = fine_ref[1]
        at = pl.multiple_of(a // per * 2 * LANES + a % per * STEP, STEP)
        inverse[pl.ds(at, STEP), :] = (cc * fc - cs * fs).astype(jnp.bfloat16)
        inverse[pl.ds(LANES + at, STEP), :] = (-(cs * fc + cc * fs)).astype(jnp.bfloat16)
        return carry

    lax.fori_loop(0, bins // STEP, fill, 0)

    span = (2 * reach + 1) * rows
    chan_a = me_chan * rows + lax.broadcasted_iota(jnp.int32, (1, rows), 1)
    chan_b = (me_chan - reach) * rows + lax.broadcasted_iota(jnp.int32, (1, span), 1)
    chan_b = jnp.where(chan_b < 0, chan_b + chan_total * rows, chan_b)
    chan_b = jnp.where(chan_b >= chan_total * rows, chan_b - chan_total * rows, chan_b)
    far = (half - 1) * group
    order = [off_peer(s) + 1 - 2 * parity for s in range(1, half)] + [off_peer(s) for s in range(1, half)]
    order += [partner, me_off]
    pairs = jnp.concatenate(
        [slots[pl.ds(pl.multiple_of(o * group, group), group), :] for o in order], axis=0
    )
    pick_a = jnp.where(pairs[:, 0:1] == chan_a, 1.0, 0.0).astype(jnp.bfloat16)
    pick_b = jnp.where(pairs[:, 1:2] == chan_b, 1.0, 0.0).astype(jnp.bfloat16)

    def product(q, lo, hi):
        left = jnp.dot(pick_a[lo:hi], table[q, reach], preferred_element_type=jnp.float32)
        right = jnp.dot(
            pick_b[lo:hi], table[q].reshape(span, 2 * LANES), preferred_element_type=jnp.float32
        )
        la, lb = left[:, :LANES], left[:, LANES:]
        ra, rb = right[:, :LANES], right[:, LANES:]
        cross = jnp.concatenate([la * ra + lb * rb, la * rb - lb * ra], axis=1).astype(jnp.bfloat16)
        return jnp.dot(
            cross, inverse[q * 2 * LANES:(q + 1) * 2 * LANES, :], preferred_element_type=jnp.float32
        )

    def swap(index, lo, count):
        copy = pltpu.make_async_remote_copy(
            src_ref=swap_send.at[pl.ds(lo, count), :],
            dst_ref=swap_recv.at[pl.ds(lo, count), :],
            send_sem=swap_send_sem.at[index],
            recv_sem=swap_recv_sem.at[index],
            device_id=(me_chan, partner),
            device_id_type=MESH,
        )
        copy.start()
        return copy

    everything = 2 * far + 2 * group
    for q in range(pieces - 1):
        for move in moves[q * len(shifts):(q + 1) * len(shifts)]:
            move.wait_recv()
        if q == 0:
            total[...] = product(q, 0, everything)
        else:
            total[...] += product(q, 0, everything)
    for move in moves[(pieces - 1) * len(shifts):]:
        move.wait_recv()

    def last(lo, hi):
        value = product(pieces - 1, lo, hi)
        return value + total[lo:hi, :] if pieces > 1 else value

    outer_rows = last(0, 2 * far)
    swap_send[:far, :] = outer_rows[:far].astype(swap_send.dtype)
    swap_far = swap(0, 0, far)
    total[far:2 * far, :] = outer_rows[far:]
    near_rows = last(2 * far, everything)
    swap_send[far:, :] = near_rows[:group].astype(swap_send.dtype)
    swap_near = swap(1, far, group)
    out_ref[...] = near_rows[group:]
    swap_far.wait_recv()
    sends = []
    for step in range(1, half):
        lo = (step - 1) * group
        sum_send[lo:lo + group, :] = (
            total[far + lo:far + lo + group, :] + swap_recv[lo:lo + group, :].astype(jnp.float32)
        ).astype(sum_send.dtype)
        send = pltpu.make_async_remote_copy(
            src_ref=sum_send.at[pl.ds(lo, group), :],
            dst_ref=sum_recv.at[pl.ds(lo, group), :],
            send_sem=off_send_sem.at[step - 1],
            recv_sem=off_recv_sem.at[step - 1],
            device_id=(me_chan, off_peer(step)),
            device_id_type=MESH,
        )
        send.start()
        sends.append(send)
    swap_near.wait_recv()
    result = out_ref[...] + swap_recv[far:, :].astype(jnp.float32)
    for step in range(1, half):
        sends[step - 1].wait_recv()
        result += sum_recv[(step - 1) * group:step * group, :].astype(jnp.float32)
    out_ref[...] = result
    for copy in moves + [swap_far, swap_near] + sends:
        copy.wait_send()


def shards(traces, band_gain, pair_list, pair_count):
    chan_total = lax.axis_size("chan")
    owners = lax.axis_size("off")
    reach = chan_total // 4
    rows, sample_count = traces.shape
    bins = band_gain.shape[0]
    group = pair_list.shape[0] // owners
    half = owners // 2
    inner = sample_count // RADIX
    all_bins = bins * owners
    assert (inner // 2) % bins == 0 and bins % LANES == 0 and half > 1

    def const(value, dtype):
        return jnp.asarray(value, dtype=dtype)

    ic, isn = angle_table(np.arange(inner), np.arange(inner // 2), inner)
    oc, osn = angle_table(np.arange(RADIX), np.arange(all_bins), sample_count)
    lag_ids = np.arange(NLAG) - NLAG // 2
    cc, cs = angle_table(np.arange(0, all_bins, STEP), lag_ids, sample_count)
    fc, fs = angle_table(np.arange(STEP), lag_ids, sample_count)
    vmem = pl.BlockSpec(memory_space=pltpu.VMEM)
    hbm = pl.BlockSpec(memory_space=pltpu.HBM)
    dma = pltpu.SemaphoreType.DMA
    peers = max(1, half - 1)
    operands = (
        traces, band_gain.reshape(1, bins), pair_list.T,
        const(np.stack([ic.reshape(inner, -1, LANES), -isn.reshape(inner, -1, LANES)], axis=2).reshape(inner, inner), jnp.bfloat16),
        const(np.concatenate([oc, -osn]), jnp.float32),
        const(np.stack([cc, cs]), jnp.float32),
        const(np.stack([fc, fs]), jnp.float32),
    )
    lagsum = pl.pallas_call(
        functools.partial(kernel, (chan_total, owners, reach)),
        out_shape=jax.ShapeDtypeStruct((group, NLAG), jnp.float32),
        in_specs=[hbm] * len(operands),
        out_specs=vmem,
        scratch_shapes=[
            *[pltpu.VMEM(x.shape, x.dtype) for x in operands],
            pltpu.VMEM(pair_list.shape, jnp.int32), dma((len(operands),)),
            pltpu.VMEM((bins // LANES, 2 * reach + 1, rows, 2 * LANES), jnp.bfloat16),
            pltpu.VMEM((2 * bins, NLAG), jnp.bfloat16),
            pltpu.VMEM((owners * group, NLAG), jnp.float32),
            pltpu.VMEM((half * group, NLAG), jnp.bfloat16),
            pltpu.VMEM((half * group, NLAG), jnp.bfloat16),
            pltpu.VMEM((peers * group, NLAG), jnp.bfloat16),
            pltpu.VMEM((peers * group, NLAG), jnp.bfloat16),
            dma((bins // LANES, 2 * reach)), dma((bins // LANES, 2 * reach)),
            dma((2,)), dma((2,)),
            dma((peers,)), dma((peers,)),
        ],
        compiler_params=pltpu.CompilerParams(
            collective_id=0, has_side_effects=True, vmem_limit_bytes=60 * 1024 * 1024
        ),
        name="correlate",
    )(*operands)
    live = jnp.arange(group, dtype=jnp.int32)[:, None] < pair_count[0]
    return jnp.where(live, lagsum * (1.0 / math.sqrt(sample_count // 2)), 0.0)


def solution(mesh):
    placed = (P("chan", None), P("off"), P("chan", None), P(("chan", "off")))
    return jax.shard_map(
        shards, mesh=mesh, in_specs=placed, out_specs=P(("chan", "off"), None), check_vma=False
    )
```

time: 28.8 us -> 27.7 us (0.962)
  other arithmetic: 0 us -> 1.75 us
  local copies, waits for them, and re-layouts: 1.67 us -> 0 us
  Pallas kernels: 26.3 us -> 25.1 us
    select_n x0 -> x1, other arithmetic: none -> 1.74 us  [shards(): return jnp.where(live, lagsum * (1.0 / math.sqrt(sample_count // 2)), 0.0)]
    unnamed x1 -> x0, local copies, waits for them, and re-layouts: 1.67 us -> none
    pallas_call x1, Pallas kernels: 26.3 us -> 25.1 us  [shards(): pl.pallas_call(functools.partial(kernel, (chan_total, owners, reach)), ou...]
where the time goes in v3:
time: 27.7 us; the launch traced here: 27.5 us
  Pallas kernels  25.1 us (91%)
  other arithmetic  1.75 us (6%)
  between operations  0.67 us (2%)
    pallas_call x1, Pallas kernels, shards(): pl.pallas_call(functools.partial(kernel, (chan_total, owners, reach)), ou...  25.1 us
    select_n x1, other arithmetic, shards(): return jnp.where(live, lagsum * (1.0 / math.sqrt(sample_count // 2)), 0.0)  1.74 us

profile of v3, /device:TPU:0, one launch (start us, length us, event | category | flops | bytes accessed | tf_op | source)
XLA Modules:
  0.0 27.5 jit_solution(8046794559689346873)
XLA Ops:
  0.7 25.1 %correlate.1 = f32[64,1024]{1,0:T(8,128)} custom-call(bf16[64,4096]{1,0:T(8,128)(2,1)} %traces_hbm.1, f32[1,512]{1,0:T(1,128)} %bitcast.4, s32[2,256]{1,0:T(2,128)} %bitcast.5, bf16[1024,1024]{1,0:T(8,128)(2,1)} %constant.12.clone.inner_hbm, f32[8,2048]{1,0:T(8,128)} %constant.13.clone.outer_hbm, f32[2,32,1024]{2,1,0:T(8,128)} %constant.14.clone.coarse_hbm, ...), custom_call_target="tpu_custom_call" | custom-call | tf_op jit(solution)/shard_map/correlate/pallas_call | solution.py:275
  25.8 1.7 %multiply_select_fusion = f32[64,1024]{1,0:T(8,128)} fusion(f32[64,1024]{1,0:T(8,128)} %correlate.1, pred[64]{0:T(512)(128)(4,1)S(1)} %iota_compare_fusion), kind=kLoop, calls=%fused_computation | loop fusion | flops 131072 | bytes 524352 | tf_op jit(solution)/shard_map/jit(_where)/select_n | solution.py:300
  (1 shorter events, 0.0 us)

commit v4 on v3

--- a/solution.py
+++ b/solution.py
@@ -14,6 +14,7 @@
 RADIX = 4
 LANES = 128
 STEP = 64
+VMEM_MIB = 58
 MESH = pl.DeviceIdType.MESH
 
 
@@ -24,9 +25,9 @@
 
 def kernel(
     sizes,
-    traces_hbm, gain_hbm, pairs_hbm, inner_hbm, outer_hbm, coarse_hbm, fine_hbm,
+    traces_hbm, gain_hbm, pairs_hbm, limit_hbm, inner_hbm, outer_hbm, coarse_hbm, fine_hbm,
     out_ref,
-    traces_ref, gain_ref, pairs_ref, inner_ref, outer_ref, coarse_ref, fine_ref, slots, load_sem,
+    traces_ref, gain_ref, pairs_ref, limit_ref, inner_ref, outer_ref, coarse_ref, fine_ref, slots, load_sem,
     table, inverse, total, swap_send, swap_recv, sum_send, sum_recv,
     chan_send_sem, chan_recv_sem, swap_send_sem, swap_recv_sem, off_send_sem, off_recv_sem,
 ):
@@ -54,7 +55,7 @@
         for i, (source, target) in enumerate(
             (
                 (traces_hbm, traces_ref), (inner_hbm, inner_ref), (outer_hbm, outer_ref), (gain_hbm, gain_ref),
-                (fine_hbm, fine_ref), (coarse_hbm, coarse_ref), (pairs_hbm, pairs_ref),
+                (fine_hbm, fine_ref), (coarse_hbm, coarse_ref), (pairs_hbm, pairs_ref), (limit_hbm, limit_ref),
             )
         )
     ]
@@ -62,6 +63,8 @@
         load.start()
 
     shifts = [s for d in range(reach, 0, -1) for s in (d, -d)]
+    relayed = pieces - 1 if reach == 2 and chan_total % 2 == 0 else 0
+    side = 1 - 2 * lax.rem(me_chan, 2)
     barrier = pltpu.get_barrier_semaphore()
     for shift in shifts:
         pl.semaphore_signal(barrier, inc=1, device_id=(chan_peer(shift), me_off), device_id_type=MESH)
@@ -74,13 +77,13 @@
     chunks = sample_count // chunk
     odd_half = lax.rem(lax.div(bin_lo, inner // 2), 2)
     src = lax.broadcasted_iota(jnp.int32, (chunk, chunk), 0)
-    dst = lax.broadcasted_iota(jnp.int32, (chunk, chunk), 1)
-    lane = lax.rem(dst, LANES)
-    wanted = RADIX * lane + lax.div(dst, LANES)
-    flip = 1.0 - 2.0 * (lax.rem(lane, 2) * odd_half).astype(jnp.float32)
+    dst = lax.broadcasted_iota(jnp.int32, (1, chunk), 1)
+    lane = jnp.bitwise_and(dst, LANES - 1)
+    wanted = RADIX * lane + jnp.right_shift(dst, LANES.bit_length() - 1)
+    flip = 1.0 - 2.0 * (jnp.bitwise_and(lane, 1) * odd_half).astype(jnp.float32)
     spread = jnp.where(src == wanted, flip, 0.0).astype(jnp.bfloat16)
-    band_a = lax.div(lax.broadcasted_iota(jnp.int32, (LANES, LANES), 0), BAND)
-    band_b = lax.div(lax.broadcasted_iota(jnp.int32, (LANES, LANES), 1), BAND)
+    band_a = jnp.right_shift(lax.broadcasted_iota(jnp.int32, (LANES, LANES), 0), BAND.bit_length() - 1)
+    band_b = jnp.right_shift(lax.broadcasted_iota(jnp.int32, (LANES, LANES), 1), BAND.bit_length() - 1)
     mean_of = jnp.where(band_a == band_b, 1.0 / BAND, 0.0).astype(jnp.bfloat16)
     loads[0].wait()
     stacked = jnp.concatenate([traces_ref[:, c * chunk:(c + 1) * chunk] for c in range(chunks)], axis=0)
@@ -97,6 +100,18 @@
     for load in loads[1:4]:
         load.wait()
     col_lo = lax.rem(bin_lo, inner // 2)
+
+    def send_block(q, i, source, target, shift):
+        move = pltpu.make_async_remote_copy(
+            src_ref=table.at[q, source],
+            dst_ref=table.at[q, target],
+            send_sem=chan_send_sem.at[q, i],
+            recv_sem=chan_recv_sem.at[q, i],
+            device_id=(chan_peer(shift), me_off),
+            device_id_type=MESH,
+        )
+        move.start()
+        return move
 
     moves = []
     for q in range(pieces):
@@ -123,17 +138,14 @@
         table[q, reach, :, LANES:] = (imag_part * scale).astype(jnp.bfloat16)
         if q == 0:
             pl.semaphore_wait(barrier, len(shifts) + half)
+        moves.append([])
         for i, shift in enumerate(shifts):
-            move = pltpu.make_async_remote_copy(
-                src_ref=table.at[q, reach],
-                dst_ref=table.at[q, reach - shift],
-                send_sem=chan_send_sem.at[q, i],
-                recv_sem=chan_recv_sem.at[q, i],
-                device_id=(chan_peer(shift), me_off),
-                device_id_type=MESH,
-            )
-            move.start()
-            moves.append(move)
+            near = q < relayed and abs(shift) == 1
+            if near and shift == -1:
+                continue
+            if near:
+                shift = side
+            moves[q].append(send_block(q, i, reach, reach - shift, shift))
 
     for load in loads[4:]:
         load.wait()
@@ -192,14 +204,18 @@
         return copy
 
     everything = 2 * far + 2 * group
+    for q in range(relayed):
+        for move in moves[q][:2]:
+            move.wait_recv()
+        moves[q].append(send_block(q, len(shifts) - 1, reach + 2 * side, reach + side, side))
     for q in range(pieces - 1):
-        for move in moves[q * len(shifts):(q + 1) * len(shifts)]:
+        for move in moves[q][2 if q < relayed else 0:]:
             move.wait_recv()
         if q == 0:
             total[...] = product(q, 0, everything)
         else:
             total[...] += product(q, 0, everything)
-    for move in moves[(pieces - 1) * len(shifts):]:
+    for move in moves[pieces - 1]:
         move.wait_recv()
 
     def last(lo, hi):
@@ -236,8 +252,9 @@
     for step in range(1, half):
         sends[step - 1].wait_recv()
         result += sum_recv[(step - 1) * group:step * group, :].astype(jnp.float32)
-    out_ref[...] = result
-    for copy in moves + [swap_far, swap_near] + sends:
+    live = lax.broadcasted_iota(jnp.int32, (group, 1), 0) < limit_ref[...]
+    out_ref[...] = jnp.where(live, result * (1.0 / math.sqrt(sample_count // 2)), 0.0)
+    for copy in [move for piece in moves for move in piece] + [swap_far, swap_near] + sends:
         copy.wait_send()
 
 
@@ -266,13 +283,13 @@
     dma = pltpu.SemaphoreType.DMA
     peers = max(1, half - 1)
     operands = (
-        traces, band_gain.reshape(1, bins), pair_list.T,
+        traces, band_gain.reshape(1, bins), pair_list.T, pair_count.reshape(1, 1),
         const(np.stack([ic.reshape(inner, -1, LANES), -isn.reshape(inner, -1, LANES)], axis=2).reshape(inner, inner), jnp.bfloat16),
         const(np.concatenate([oc, -osn]), jnp.float32),
         const(np.stack([cc, cs]), jnp.float32),
         const(np.stack([fc, fs]), jnp.float32),
     )
-    lagsum = pl.pallas_call(
+    return pl.pallas_call(
         functools.partial(kernel, (chan_total, owners, reach)),
         out_shape=jax.ShapeDtypeStruct((group, NLAG), jnp.float32),
         in_specs=[hbm] * len(operands),
@@ -292,12 +309,10 @@
             dma((peers,)), dma((peers,)),
         ],
         compiler_params=pltpu.CompilerParams(
-            collective_id=0, has_side_effects=True, vmem_limit_bytes=60 * 1024 * 1024
+            collective_id=0, has_side_effects=True, vmem_limit_bytes=int(VMEM_MIB * 1024 * 1024)
         ),
         name="correlate",
     )(*operands)
-    live = jnp.arange(group, dtype=jnp.int32)[:, None] < pair_count[0]
-    return jnp.where(live, lagsum * (1.0 / math.sqrt(sample_count // 2)), 0.0)
 
 
 def solution(mesh):

time: 27.7 us -> 26.6 us (0.960)
  other arithmetic: 1.75 us -> 0 us
  local copies, waits for them, and re-layouts: 0 us -> 1.67 us
  Pallas kernels: 25.1 us -> 24.1 us
    select_n x1 -> x0, other arithmetic: 1.74 us -> none  [shards(): return jnp.where(live, lagsum * (1.0 / math.sqrt(sample_count // 2)), 0.0)]
    unnamed x0 -> x1, local copies, waits for them, and re-layouts: none -> 1.67 us
    pallas_call x1, Pallas kernels: 25.1 us -> 24.1 us  [shards(): pl.pallas_call(functools.partial(kernel, (chan_total, owners, reach)), ou...]
where the time goes in v4:
time: 26.6 us; the launch traced here: 26.4 us
  Pallas kernels  24.1 us (91%)
  local copies, waits for them, and re-layouts  1.67 us (6%)
  between operations  0.66 us (2%)
    pallas_call x1, Pallas kernels, shards(): pl.pallas_call(functools.partial(kernel, (chan_total, owners, reach)), ou...  24.1 us
    unnamed x1, local copies, waits for them, and re-layouts  1.67 us

profile of v4, /device:TPU:0, one launch (start us, length us, event | category | flops | bytes accessed | tf_op | source)
XLA Modules:
  0.0 26.4 jit_solution(11859438245850821902)
XLA Ops:
  0.7 24.1 %correlate.1 = f32[64,1024]{1,0:T(8,128)} custom-call(bf16[64,4096]{1,0:T(8,128)(2,1)} %traces_hbm.1, f32[1,512]{1,0:T(1,128)} %bitcast.4, s32[2,256]{1,0:T(2,128)} %bitcast.5, s32[1,1]{1,0:T(1,128)} %bitcast.3.limit_hbm, bf16[1024,1024]{1,0:T(8,128)(2,1)} %constant.8.clone.inner_hbm, f32[8,2048]{1,0:T(8,128)} %constant.9.clone.outer_hbm, ...), custom_call_target="tpu_custom_call" | custom-call | tf_op jit(solution)/shard_map/correlate/pallas_call | solution.py:292
  24.7 1.7 %copy.11 = f32[64,1024]{1,0:T(8,128)} copy(f32[64,1024]{1,0:T(8,128)} %correlate.1) | data formatting | bytes 524288

commit v5 on v4

--- a/solution.py
+++ b/solution.py
@@ -291,7 +291,7 @@
     )
     return pl.pallas_call(
         functools.partial(kernel, (chan_total, owners, reach)),
-        out_shape=jax.ShapeDtypeStruct((group, NLAG), jnp.float32),
+        out_shape=pltpu.VMEM((group, NLAG), jnp.float32),
         in_specs=[hbm] * len(operands),
         out_specs=vmem,
         scratch_shapes=[

time: 26.6 us -> 24.9 us (0.936)
  local copies, waits for them, and re-layouts: 1.67 us -> 0.71 us
  Pallas kernels: 24.1 us -> 23.4 us
    unnamed x1, local copies, waits for them, and re-layouts: 1.67 us -> 0.71 us
    pallas_call x1, Pallas kernels: 24.1 us -> 23.4 us  [shards(): pl.pallas_call(functools.partial(kernel, (chan_total, owners, reach)), ou...]
where the time goes in v5:
time: 24.9 us; the launch traced here: 24.8 us
  Pallas kernels  23.4 us (94%)
  local copies, waits for them, and re-layouts  0.71 us (3%)
  between operations  0.66 us (3%)
    pallas_call x1, Pallas kernels, shards(): pl.pallas_call(functools.partial(kernel, (chan_total, owners, reach)), ou...  23.4 us
    unnamed x1, local copies, waits for them, and re-layouts  0.71 us

profile of v5, /device:TPU:0, one launch (start us, length us, event | category | flops | bytes accessed | tf_op | source)
XLA Modules:
  0.0 24.8 jit_solution(13778447303387855833)
XLA Ops:
  0.7 23.4 %correlate.1 = f32[64,1024]{1,0:T(8,128)S(1)} custom-call(bf16[64,4096]{1,0:T(8,128)(2,1)} %traces_hbm.1, f32[1,512]{1,0:T(1,128)} %bitcast.4, s32[2,256]{1,0:T(2,128)} %bitcast.5, s32[1,1]{1,0:T(1,128)} %bitcast.3.limit_hbm, bf16[1024,1024]{1,0:T(8,128)(2,1)} %constant.8.clone.inner_hbm, f32[8,2048]{1,0:T(8,128)} %constant.9.clone.outer_hbm, ...), custom_call_target="tpu_custom_call" | custom-call | tf_op jit(solution)/shard_map/correlate/pallas_call | solution.py:292
  24.1 0.7 %copy.10 = f32[64,1024]{1,0:T(8,128)} copy(f32[64,1024]{1,0:T(8,128)S(1)} %correlate.1) | data formatting | bytes 524288
